TPU v7x, 128 devices: a whole 4x4x4 slice. The times are simulated.
128 devices in a mesh: dp: 8 (over z, core), seq: 16 (over x, y).
Axes of the slice: x: 4, y: 4, z: 4, core: 2. Of those that a mesh axis runs over, the one named last changes fastest.
Arguments:
- dec_input: bfloat16 [128, 128, 768], P(('dp', 'seq')), may hold values from -6 to 6
- memory: bfloat16 [128, 3072, 768], P('dp', 'seq'), may hold values from -6 to 6
- mem_len: int32 [128], P(('dp', 'seq')), may hold values from 1 to 3072, 196608 in all
- grad_out: bfloat16 [128, 128, 768], P(('dp', 'seq')), may hold values from -6 to 6
- attn_master: float32 [8, 768, 768], P(None, ('dp', 'seq'))
- ffn_in_master: float32 [2, 768, 2048], P(None, ('dp', 'seq')), may hold values from -0.21875 to 0.21875
- ffn_out_master: float32 [2048, 768], P(('dp', 'seq')), may hold values from -0.125 to 0.125
- gain_master: float32 [3, 768], P(None, ('dp', 'seq')), may hold values from 0.5 to 1.5
- attn_first: float32 [8, 768, 768], P(None, ('dp', 'seq')), may hold values from -64 to 64
- ffn_in_first: float32 [2, 768, 2048], P(None, ('dp', 'seq')), may hold values from -40 to 40
- ffn_out_first: float32 [2048, 768], P(('dp', 'seq')), may hold values from -40 to 40
- gain_first: float32 [3, 768], P(None, ('dp', 'seq')), may hold values from -96 to 96
- attn_second: float32 [8, 768, 768], P(None, ('dp', 'seq'))
- ffn_in_second: float32 [2, 768, 2048], P(None, ('dp', 'seq')), may hold values from 4.096 to 16.384
- ffn_out_second: float32 [2048, 768], P(('dp', 'seq')), may hold values from 4.096 to 16.384
- gain_second: float32 [3, 768], P(None, ('dp', 'seq'))
Outputs:
- out_block: bfloat16 [128, 128, 768], P(('dp', 'seq'))
- grad_input: float32 [128, 128, 768], P(('dp', 'seq'))
- grad_memory: float32 [128, 3072, 768], P('dp', 'seq')
- attn_new: float32 [8, 768, 768], P(None, ('dp', 'seq'))
- attn_first_new: float32 [8, 768, 768], P(None, ('dp', 'seq'))
- attn_second_new: float32 [8, 768, 768], P(None, ('dp', 'seq'))
- attn_copy: bfloat16 [8, 768, 768], P(None, ('dp', 'seq'))
- ffn_in_new: float32 [2, 768, 2048], P(None, ('dp', 'seq'))
- ffn_in_first_new: float32 [2, 768, 2048], P(None, ('dp', 'seq'))
- ffn_in_second_new: float32 [2, 768, 2048], P(None, ('dp', 'seq'))
- ffn_in_copy: bfloat16 [2, 768, 2048], P(None, ('dp', 'seq'))
- ffn_out_new: float32 [2048, 768], P(('dp', 'seq'))
- ffn_out_first_new: float32 [2048, 768], P(('dp', 'seq'))
- ffn_out_second_new: float32 [2048, 768], P(('dp', 'seq'))
- ffn_out_copy: bfloat16 [2048, 768], P(('dp', 'seq'))
- gain_new: float32 [3, 768], P(None, ('dp', 'seq'))
- gain_first_new: float32 [3, 768], P(None, ('dp', 'seq'))
- gain_second_new: float32 [3, 768], P(None, ('dp', 'seq'))
- gain_copy: bfloat16 [3, 768], P(None, ('dp', 'seq'))
Inputs may be any that keep to these rules, and one draw needn't show every extreme that they name: `mem_len`: each example's count of live memory positions; the largest is exactly 3072.
All inputs are finite; a program needn't handle non-finite values. No bound on the sum of `mem_len` on one device may be relied on, other than what follows from the above.
Results may differ from a plain program's by a relative error of at most 0.02.
The roundings to bfloat16 on the way count: a program that leaves them out, or rounds other values in their place, can miss the bound.
Values may be sent and summed in bfloat16 or wider, within the bound.
A program may use at most 256 MiB of HBM per device.

v0:
```python
import jax
import jax.numpy as jnp
from jax import lax
from jax.sharding import PartitionSpec as P

H = 12
HEAD = 64
STEP = 10


eps_norm = 1e-06
score_scale = 0.125
beta_one = 0.9
beta_two = 0.999
adam_eps = 1e-08
decay_rate = 0.01
rate_matrix = 0.12
rate_gain = 3.0
neg_big = -1e30


def dense(left, right):
    return jnp.dot(left, right, preferred_element_type=jnp.float32)


def weight_grad(left, right):
    return jnp.einsum("rd,re->de", left, right, preferred_element_type=jnp.float32)


def back_dense(incoming, weight):
    return jnp.einsum("re,de->rd", incoming, weight, preferred_element_type=jnp.float32)


def gated_gelu(gate_part, up_part):
    return jax.nn.gelu(gate_part, approximate=True) * up_part


def norm_forward(tok_rows, gain_row):
    inverse = lax.rsqrt(jnp.mean(tok_rows * tok_rows, axis=-1, keepdims=True) + eps_norm)
    return ((tok_rows * inverse * gain_row).astype(jnp.bfloat16), inverse)


def norm_backward(tok_rows, inverse, gain_row, incoming):
    scaled = incoming * gain_row
    gain_grad = jnp.sum(incoming * tok_rows * inverse, axis=0)
    inner_sum = jnp.mean(scaled * tok_rows, axis=-1, keepdims=True)
    return (inverse * scaled - tok_rows * inverse * inverse * inverse * inner_sum, gain_grad)


def scores_of(queries, key_set, is_valid):
    scores = (
        jnp.einsum("eqhc,ekhc->ehqk", queries, key_set, preferred_element_type=jnp.float32)
        * score_scale
    )
    return jnp.where(is_valid, scores, neg_big)


def attend_forward(queries, key_set, values, is_valid):
    scores = scores_of(queries, key_set, is_valid)
    row_top = jnp.max(scores, axis=-1, keepdims=True)
    logsum = row_top + jnp.log(jnp.sum(jnp.exp(scores - row_top), axis=-1, keepdims=True))
    prob_rows = jnp.exp(scores - logsum).astype(jnp.bfloat16)
    mixed = jnp.einsum("ehqk,ekhc->eqhc", prob_rows, values, preferred_element_type=jnp.float32)
    return (mixed.astype(jnp.bfloat16), logsum)


def attend_backward(queries, key_set, values, is_valid, logsum, incoming):
    prob_rows = jnp.exp(scores_of(queries, key_set, is_valid) - logsum)
    value_grad = jnp.einsum(
        "ehqk,eqhc->ekhc",
        prob_rows.astype(jnp.bfloat16),
        incoming,
        preferred_element_type=jnp.float32,
    )
    prob_grad = jnp.einsum("eqhc,ekhc->ehqk", incoming, values, preferred_element_type=jnp.float32)
    row_delta = jnp.sum(prob_grad * prob_rows, axis=-1, keepdims=True)
    score_grad = (prob_rows * (prob_grad - row_delta)).astype(jnp.bfloat16)
    query_grad = (
        jnp.einsum("ehqk,ekhc->eqhc", score_grad, key_set, preferred_element_type=jnp.float32)
        * score_scale
    )
    key_grad = (
        jnp.einsum("ehqk,eqhc->ekhc", score_grad, queries, preferred_element_type=jnp.float32)
        * score_scale
    )
    return (
        query_grad.astype(jnp.bfloat16),
        key_grad.astype(jnp.bfloat16),
        value_grad.astype(jnp.bfloat16),
    )


def adam_update(master, first, second, grad, rate):
    first_new = beta_one * first + (1.0 - beta_one) * grad
    second_new = beta_two * second + (1.0 - beta_two) * grad * grad
    fix_one = 1.0 - beta_one**STEP
    fix_two = 1.0 - beta_two**STEP
    master_new = master - rate * (
        first_new / fix_one / (jnp.sqrt(second_new / fix_two) + adam_eps) + decay_rate * master
    )
    return (master_new, first_new, second_new, master_new.astype(jnp.bfloat16))


def body(
    dec_input,
    memory,
    mem_len,
    grad_out,
    attn_master,
    ffn_in_master,
    ffn_out_master,
    gain_master,
    attn_first,
    ffn_in_first,
    ffn_out_first,
    gain_first,
    attn_second,
    ffn_in_second,
    ffn_out_second,
    gain_second,
):
    attn_w, in_w, out_w, gain_w = (
        lax.all_gather(attn_master.astype(jnp.bfloat16), ("dp", "seq"), axis=1, tiled=True),
        lax.all_gather(ffn_in_master.astype(jnp.bfloat16), ("dp", "seq"), axis=1, tiled=True),
        lax.all_gather(ffn_out_master.astype(jnp.bfloat16), ("dp", "seq"), axis=0, tiled=True),
        lax.all_gather(gain_master.astype(jnp.bfloat16), ("dp", "seq"), axis=1, tiled=True),
    )
    gains = gain_w.astype(jnp.float32)
    examples, tgt_len, width = dec_input.shape
    total_rows = examples * tgt_len

    def split_heads(block):
        return block.reshape(examples, -1, H, HEAD)

    tok_rows = dec_input.astype(jnp.float32).reshape(total_rows, width)
    h_one, inv_one = norm_forward(tok_rows, gains[0])
    triple = jnp.einsum(
        "rd,kde->kre", h_one, attn_w[0:3], preferred_element_type=jnp.float32
    ).astype(jnp.bfloat16)
    q_one = split_heads(triple[0])
    k_one = split_heads(triple[1])
    v_one = split_heads(triple[2])
    position = jnp.arange(tgt_len)
    causal = (position[:, None] >= position[None, :])[None, None]
    mixed_one, lse_one = attend_forward(q_one, k_one, v_one, causal)
    flat_one = mixed_one.reshape(total_rows, width)
    after_one = tok_rows + dense(flat_one, attn_w[3])
    h_two, inv_two = norm_forward(after_one, gains[1])
    q_two = split_heads(dense(h_two, attn_w[4]).astype(jnp.bfloat16))
    local_pair = jnp.einsum(
        "emd,kdf->kemf", memory, attn_w[5:7], preferred_element_type=jnp.float32
    ).astype(jnp.bfloat16)
    pair = lax.all_to_all(local_pair, "seq", split_axis=1, concat_axis=2, tiled=True)
    mem_pos = jnp.arange(pair.shape[2])
    reach = (mem_pos[None, :] < mem_len[:, None])[:, None, None, :]
    k_two = split_heads(pair[0])
    v_two = split_heads(pair[1])
    mixed_two, lse_two = attend_forward(q_two, k_two, v_two, reach)
    flat_two = mixed_two.reshape(total_rows, width)
    after_two = after_one + dense(flat_two, attn_w[7])
    h_three, inv_three = norm_forward(after_two, gains[2])
    gate_up = jnp.einsum("rd,kdf->krf", h_three, in_w, preferred_element_type=jnp.float32)
    middle = gated_gelu(gate_up[0], gate_up[1]).astype(jnp.bfloat16)
    result = after_two + dense(middle, out_w)
    out_block = result.astype(jnp.bfloat16).reshape(dec_input.shape)
    grad_rows = grad_out.astype(jnp.float32).reshape(total_rows, width)
    grad_low = grad_rows.astype(jnp.bfloat16)
    g_down = jnp.einsum("rf,rd->fd", middle, grad_low, preferred_element_type=jnp.float32)
    grad_mid = jnp.einsum("rd,fd->rf", grad_low, out_w, preferred_element_type=jnp.float32)
    unused_value, pull = jax.vjp(gated_gelu, gate_up[0], gate_up[1])
    grad_gate, grad_up = pull(grad_mid)
    grad_pair = jnp.stack([grad_gate, grad_up]).astype(jnp.bfloat16)
    g_up = jnp.einsum("rd,krf->kdf", h_three, grad_pair, preferred_element_type=jnp.float32)
    grad_h_three = jnp.einsum("krf,kdf->rd", grad_pair, in_w, preferred_element_type=jnp.float32)
    norm_three, gain_three = norm_backward(after_two, inv_three, gains[2], grad_h_three)
    grad_two = grad_rows + norm_three
    cross_low = grad_two.astype(jnp.bfloat16)
    g_cross_out = weight_grad(flat_two, cross_low)
    grad_mixed_two = split_heads(back_dense(cross_low, attn_w[7]).astype(jnp.bfloat16))
    dq_two, dk_two, dv_two = attend_backward(q_two, k_two, v_two, reach, lse_two, grad_mixed_two)
    dq_flat = dq_two.reshape(total_rows, width)
    g_cross_query = weight_grad(h_two, dq_flat)
    kv_grad = jnp.stack([dk_two.reshape(examples, -1, width), dv_two.reshape(examples, -1, width)])
    kv_back = lax.all_to_all(kv_grad, "seq", split_axis=2, concat_axis=1, tiled=True)
    g_cross_kv = jnp.einsum("emd,kemf->kdf", memory, kv_back, preferred_element_type=jnp.float32)
    grad_memory = jnp.einsum(
        "kemf,kdf->emd", kv_back, attn_w[5:7], preferred_element_type=jnp.float32
    )
    norm_two, gain_two = norm_backward(after_one, inv_two, gains[1], back_dense(dq_flat, attn_w[4]))
    grad_one = grad_two + norm_two
    self_low = grad_one.astype(jnp.bfloat16)
    g_self_out = weight_grad(flat_one, self_low)
    grad_mixed_one = split_heads(back_dense(self_low, attn_w[3]).astype(jnp.bfloat16))
    dq_one, dk_one, dv_one = attend_backward(q_one, k_one, v_one, causal, lse_one, grad_mixed_one)
    grad_triple = jnp.stack(
        [
            dq_one.reshape(total_rows, width),
            dk_one.reshape(total_rows, width),
            dv_one.reshape(total_rows, width),
        ]
    )
    g_self_qkv = jnp.einsum("rd,kre->kde", h_one, grad_triple, preferred_element_type=jnp.float32)
    grad_h_one = jnp.einsum(
        "kre,kde->rd", grad_triple, attn_w[0:3], preferred_element_type=jnp.float32
    )
    norm_one, gain_one = norm_backward(tok_rows, inv_one, gains[0], grad_h_one)
    grad_input = (grad_one + norm_one).reshape(dec_input.shape)
    g_attn = jnp.concatenate(
        [g_self_qkv, g_self_out[None], g_cross_query[None], g_cross_kv, g_cross_out[None]], axis=0
    )
    g_gain = jnp.stack([gain_one, gain_two, gain_three])
    summed = lax.psum((g_attn, g_up, g_down, g_gain), ("dp", "seq"))
    owner = lax.axis_index(("dp", "seq"))
    shares = (
        lax.dynamic_slice_in_dim(summed[0], owner * attn_master.shape[1], attn_master.shape[1], 1),
        lax.dynamic_slice_in_dim(
            summed[1], owner * ffn_in_master.shape[1], ffn_in_master.shape[1], 1
        ),
        lax.dynamic_slice_in_dim(
            summed[2], owner * ffn_out_master.shape[0], ffn_out_master.shape[0], 0
        ),
        lax.dynamic_slice_in_dim(summed[3], owner * gain_master.shape[1], gain_master.shape[1], 1),
    )
    attn_res = adam_update(attn_master, attn_first, attn_second, shares[0], rate_matrix)
    in_res = adam_update(ffn_in_master, ffn_in_first, ffn_in_second, shares[1], rate_matrix)
    out_res = adam_update(ffn_out_master, ffn_out_first, ffn_out_second, shares[2], rate_matrix)
    gain_res = adam_update(gain_master, gain_first, gain_second, shares[3], rate_gain)
    return (
        out_block,
        grad_input,
        grad_memory,
        attn_res[0],
        attn_res[1],
        attn_res[2],
        attn_res[3],
        in_res[0],
        in_res[1],
        in_res[2],
        in_res[3],
        out_res[0],
        out_res[1],
        out_res[2],
        out_res[3],
        gain_res[0],
        gain_res[1],
        gain_res[2],
        gain_res[3],
    )


def solution(mesh):
    placed = (
        P(("dp", "seq"), None, None),
        P("dp", "seq", None),
        P(("dp", "seq")),
        P(("dp", "seq"), None, None),
        P(None, ("dp", "seq"), None),
        P(None, ("dp", "seq"), None),
        P(("dp", "seq"), None),
        P(None, ("dp", "seq")),
        P(None, ("dp", "seq"), None),
        P(None, ("dp", "seq"), None),
        P(("dp", "seq"), None),
        P(None, ("dp", "seq")),
        P(None, ("dp", "seq"), None),
        P(None, ("dp", "seq"), None),
        P(("dp", "seq"), None),
        P(None, ("dp", "seq")),
    )
    return jax.shard_map(
        body,
        mesh=mesh,
        in_specs=placed,
        out_specs=(
            P(("dp", "seq"), None, None),
            P(("dp", "seq"), None, None),
            P("dp", "seq", None),
            P(None, ("dp", "seq"), None),
            P(None, ("dp", "seq"), None),
            P(None, ("dp", "seq"), None),
            P(None, ("dp", "seq"), None),
            P(None, ("dp", "seq"), None),
            P(None, ("dp", "seq"), None),
            P(None, ("dp", "seq"), None),
            P(None, ("dp", "seq"), None),
            P(("dp", "seq"), None),
            P(("dp", "seq"), None),
            P(("dp", "seq"), None),
            P(("dp", "seq"), None),
            P(None, ("dp", "seq")),
            P(None, ("dp", "seq")),
            P(None, ("dp", "seq")),
            P(None, ("dp", "seq")),
        ),
        check_vma=False,
    )
```

profile of v0, /device:TPU:0, one launch (start us, length us, event | category | flops | bytes accessed | tf_op | source)
XLA Modules:
  0.0 1129.6 jit_solution(12861036312684109285)
XLA Ops:
  7.2 1.6 convert_element_type.172
  8.9 1.6 convert_element_type.188
  10.4 74.5 %all-gather.5.cloned.1.call-done = bf16[8,768,768]{2,0,1:T(8,128)(2,1)} async-done(((bf16[8,6,768]{2,0,1:T(8,128)(2,1)}), bf16[8,768,768]{2,0,1:T(8,128)(2,1)}) %all-gather.5.cloned.1.call-update) | async-done | bytes 9437200 | tf_op jit(solution)/shard_map/all_gather | solution.py:123
  85.0 6.1 slice.79
  91.1 1.4 copy-done.23
  92.5 11.8 %convert_bitcast_fusion = bf16[2,16,192,768]{3,2,1,0:T(8,128)(2,1)} fusion(bf16[16,192,768]{2,1,0:T(8,128)(2,1)} %param.17, bf16[2,768,768]{2,0,1:T(2,128)(2,1)S(1)} %slice.79), kind=kOutput, calls=%fused_computation.9 | convolution fusion | flops 7252475904 | bytes 16515072 | tf_op jit(solution)/shard_map/emd,kdf->kemf/dot_general | solution.py:150
  104.3 8.3 copy.274
  112.7 4.9 all-to-all-start
  118.4 211.2 %all-gather = bf16[128,6,3]{1,2,0:T(4,128)(2,1)S(1)} all-gather(bf16[1,6,3]{1,2,0:T(4,128)(2,1)S(1)} %convert_bitcast_fusion.1), channel_id=1, replica_groups=mesh['dp'=8,'seq'=16] {'dp','seq'}, dimensions={0}, use_global_device_ids=true | all-gather | bytes 4644 | tf_op jit(solution)/shard_map/all_gather | solution.py:126
  331.5 4.9 slice.74
  336.4 2.2 copy-done.15
  340.6 16.2 %fusion.129 = (bf16[1,768,768]{2,0,1:T(2,128)(2,1)S(1)}, bf16[1,768,768]{2,0,1:T(2,128)(2,1)S(1)}, bf16[1,768,768]{2,0,1:T(2,128)(2,1)S(1)}) fusion(bf16[8,768,768]{2,0,1:T(8,128)(2,1)} %all-gather.5.cloned.1.call-done), kind=kLoop, calls=%fused_computation.185 | loop fusion | bytes 7077888 | tf_op jit(solution)/shard_map/slice | solution.py:160
  357.2 1.3 copy-done.1
  360.5 8.5 fusion.130
  369.0 9.1 copy.275
  378.1 10.7 reshape.313
  388.7 9.1 copy.278
  397.8 10.9 reshape.315
  408.7 11.6 %fusion = (f32[12,128]{1,0:T(8,128)S(1)}, f32[12,128,3072]{2,1,0:T(8,128)}) fusion(pred[3072]{0:T(1024)(128)(4,1)S(1)} %iota_compare_fusion.1, bf16[128,12,64]{0,2,1:T(8,128)(2,1)S(1)} %bitcast.219, bf16[3072,12,64]{0,2,1:T(8,128)(2,1)} %reshape.315), kind=kOutput, calls=%fused_computation.5 | convolution fusion | flops 618134016 | bytes 23798784 | tf_op jit(solution)/shard_map/eqhc,ekhc->ehqk/dot_general | solution.py:52
  420.3 10.4 exponential_reduce_fusion
  430.7 12.0 %convolution_convert_fusion.1 = bf16[12,64,128]{2,1,0:T(8,128)(2,1)S(1)} fusion(bf16[3072,12,64]{0,2,1:T(8,128)(2,1)} %reshape.313, f32[12,128,3072]{2,1,0:T(8,128)} %get-tuple-element.138, f32[12,128]{1,0:T(8,128)S(1)} %log_add_fusion, pred[3072]{0:T(1024)(128)(4,1)S(1)} %iota_compare_fusion.1), kind=kOutput, calls=%fused_computation.45 | convolution fusion | flops 622952448 | bytes 23798784 | tf_op jit(solution)/shard_map/ehqk,ekhc->eqhc/dot_general | solution.py:63
  443.4 7.2 fusion.9
  450.6 3.5 fusion.66
  454.3 3.6 multiply_reduce_fusion.2
  459.0 1.2 convolution_convert_fusion.4
  461.3 14.4 %multiply_reduce_fusion = (f32[12,128]{1,0:T(8,128)S(1)}, f32[12,128,3072]{2,1,0:T(8,128)}) fusion(f32[12,128,3072]{2,1,0:T(8,128)} %get-tuple-element.138, f32[12,128]{1,0:T(8,128)S(1)} %copy-done.51, pred[3072]{0:T(1024)(128)(4,1)S(1)} %iota_compare_fusion.1, bf16[128,12,64]{0,2,1:T(8,128)(2,1)S(1)} %bitcast.221, bf16[3072,12,64]{0,2,1:T(8,128)(2,1)} %reshape.313), kind=kOutput, calls=%fused_computation.1 | convolution fusion | flops 627571200 | bytes 42679296 | tf_op jit(solution)/shard_map/eqhc,ekhc->ehqk/dot_general | solution.py:75
  475.7 10.3 convolution_convert_fusion
  486.0 20.4 %copy.291 = bf16[1,1,3072,768]{3,0,1,2:T(2,128)(2,1)} copy(bf16[1,1,3072,768]{2,3,1,0:T(8,128)(2,1)} %bitcast.216) | data formatting | bytes 9437184 | tf_op jit(solution)/shard_map/stack;reshape | solution.py:183
  506.4 13.6 %multiply_convert_fusion = bf16[12,128,3072]{2,1,0:T(8,128)(2,1)S(1)} fusion(f32[12,128,3072]{2,1,0:T(8,128)} %get-tuple-element.143, f32[12,128,3072]{2,1,0:T(8,128)} %get-tuple-element.138, f32[12,128]{1,0:T(8,128)S(1)} %get-tuple-element.142, f32[12,128]{1,0:T(8,128)S(1)} %copy-done.51, pred[3072]{0:T(1024)(128)(4,1)S(1)} %iota_compare_fusion.1), kind=kLoop, calls=%fused_computation | loop fusion | flops 28311552 | bytes 47201280 | tf_op jit(solution)/shard_map/convert_element_type | solution.py:77
  520.1 3.6 multiply_convert_fusion.1
  523.7 1.6 copy-done
  525.3 20.4 %copy.290 = bf16[1,1,3072,768]{3,0,1,2:T(2,128)(2,1)} copy(bf16[1,1,3072,768]{2,3,1,0:T(8,128)(2,1)} %bitcast.214) | data formatting | bytes 9437184 | tf_op jit(solution)/shard_map/stack;reshape | solution.py:183
  545.7 22.2 %pad_maximum_fusion = bf16[2,1,3072,768]{3,0,1,2:T(2,128)(2,1)} fusion(bf16[1,1,3072,768]{3,0,1,2:T(2,128)(2,1)} %copy.291, bf16[1,1,3072,768]{3,0,1,2:T(2,128)(2,1)} %copy.290), kind=kLoop, calls=%fused_computation.7 | loop fusion | flops 18874368 | bytes 18874368 | tf_op jit(solution)/shard_map/stack | solution.py:183
  567.8 4.8 all-to-all-start.1
  572.8 8.6 fusion.32
  583.7 1.2 convolution_convert_fusion.3
  585.0 1.7 copy.283
  586.7 2.0 convolution_convert_fusion.2
  588.7 1.7 copy.289
  590.4 1.3 multiply_reduce_fusion.1
  592.7 1.3 fusion.35
  594.2 1.4 fusion.34
  596.4 4.9 fusion.82
  601.4 11.1 copy.294
  612.9 3.0 broadcast_in_dim.63
  616.5 3.0 broadcast_in_dim.64
  620.0 3.0 broadcast_in_dim.65
  623.0 6.4 fusion.56
  629.4 19.4 %copy.297 = f32[2,2048,768]{1,0,2:T(2,128)} copy(f32[2,2048,768]{2,1,0:T(8,128)} %fusion.56) | data formatting | bytes 25165824 | tf_op jit(solution)/shard_map/rd,krf->kdf/dot_general | solution.py:173
  648.9 3.8 fusion.60
  652.6 83.4 %all-to-all-done.1 = bf16[2,1,3072,768]{3,0,1,2:T(2,128)(2,1)} async-done(((bf16[2,1,3072,768]{3,0,1,2:T(2,128)(2,1)}), bf16[2,1,3072,768]{3,0,1,2:T(2,128)(2,1)}, u32[]{:S(2)}, u32[]{:S(2)}) %all-to-all-start.1) | async-done | bytes 9437216 | tf_op jit(solution)/shard_map/all_to_all | solution.py:184
  736.1 8.5 copy.292
  744.5 13.2 %fusion.16 = f32[2,768,768]{2,1,0:T(8,128)} fusion(bf16[2,16,192,768]{3,2,1,0:T(8,128)(2,1)} %bitcast.217, bf16[16,192,768]{2,1,0:T(8,128)(2,1)} %param.17), kind=kOutput, calls=%fused_computation.25 | convolution fusion | flops 7247757312 | bytes 18874368 | tf_op jit(solution)/shard_map/emd,kemf->kdf/dot_general | solution.py:185
  757.8 8.2 copy.295
  766.0 48.4 %concatenate.3 = f32[8,768,768]{2,0,1:T(8,128)} concatenate(f32[3,768,768]{2,0,1:T(4,128)} %bitcast.213, f32[1,768,768]{2,0,1:T(1,128)} %broadcast_in_dim.63, f32[1,768,768]{2,0,1:T(1,128)} %broadcast_in_dim.64, f32[2,768,768]{2,0,1:T(2,128)} %bitcast.215, f32[1,768,768]{2,0,1:T(1,128)} %broadcast_in_dim.65), dimensions={0} | concatenate | bytes 37748736 | tf_op jit(solution)/shard_map/concatenate | solution.py:208
  815.4 4.5 fusion.79
  820.0 71.4 %psum.31 = f32[3,768]{1,0:T(4,128)S(1)} all-reduce(f32[3,768]{1,0:T(4,128)S(1)} %pad_maximum_fusion.7), channel_id=1, replica_groups=mesh['dp'=8,'seq'=16] {'dp','seq'}, use_global_device_ids=true, to_apply=%region_18.19 | all-reduce | flops 2304 | bytes 18432 | tf_op jit(solution)/shard_map/psum | solution.py:212
  892.1 2.2 fusion.75
  894.3 4.0 fusion.36
  898.4 12.7 %convolution_bitcast_fusion = f32[16,192,768]{2,1,0:T(8,128)} fusion(bf16[2,16,192,768]{3,2,1,0:T(8,128)(2,1)} %bitcast.218, bf16[2,768,768]{2,0,1:T(2,128)(2,1)S(1)} %copy-done.24), kind=kOutput, calls=%fused_computation.18 | convolution fusion | flops 7247757312 | bytes 21233664 | tf_op jit(solution)/shard_map/kemf,kdf->emd/dot_general | solution.py:186
  911.1 206.3 %all-reduce.3.cloned.1.call-done = (f32[8,768,768]{2,0,1:T(8,128)}, f32[2,768,2048]{2,0,1:T(2,128)}, f32[2048,768]{1,0:T(8,128)}) async-done(((f32[8,768,768]{2,0,1:T(8,128)}, f32[2,768,2048]{2,0,1:T(2,128)}, f32[2048,768]{1,0:T(8,128)}), (f32[8,768,768]{2,0,1:T(8,128)}, f32[2,768,2048]{2,0,1:T(2,128)}, f32[2048,768]{1,0:T(8,128)})) %all-reduce.3.cloned.1.call-update) | async-done | bytes 37748752 | tf_op jit(solution)/shard_map/psum | solution.py:212
  1117.4 1.8 fusion.127
  1119.2 1.9 fusion.125
  1121.2 1.5 fusion.123
  (187 shorter events, 16.6 us)
Async XLA Ops:
  7.2 77.8 %all-gather.5.cloned.1.call-start = ((), (), s32[]{:S(2)}) async-start(), calls=%async_computation.2 | async-start | bytes 9510912 | tf_op jit(solution)/shard_map/all_gather | solution.py:123
  8.8 434.5 %all-gather.7.cloned.1.call-start = ((), (), s32[]{:S(2)}) async-start(), calls=%async_computation.3 | async-start | bytes 6340608 | tf_op jit(solution)/shard_map/all_gather | solution.py:124
  91.1 1.4 copy-start.23
  112.7 5.0 copy-start.46
  112.7 5.7 copy-start.60
  112.7 218.7 %copy-start.19 = (bf16[1,128,768]{2,1,0:T(8,128)(2,1)S(1)}, bf16[1,128,768]{2,1,0:T(8,128)(2,1)}, u32[]{:S(2)}) copy-start(bf16[1,128,768]{2,1,0:T(8,128)(2,1)} %param.16) | copy-start | bytes 589828
  112.7 247.8 %all-to-all-start = ((bf16[2,16,192,768]{3,2,0,1:T(8,128)(2,1)}), bf16[2,16,192,768]{3,2,0,1:T(8,128)(2,1)}, u32[]{:S(2)}, u32[]{:S(2)}) async-start(bf16[2,16,192,768]{3,2,0,1:T(8,128)(2,1)} %copy.274), calls=%async_computation | async-start | bytes 18874368 | tf_op jit(solution)/shard_map/all_to_all | solution.py:153
  117.6 333.0 %all-gather.9.cloned.1.call-start = ((), (), s32[]{:S(2)}) async-start(), calls=%async_computation.4 | async-start | bytes 3170304 | tf_op jit(solution)/shard_map/all_gather | solution.py:125
  331.3 8.0 copy-start.56
  331.5 7.9 copy-start.62
  336.4 2.2 copy-start.15
  339.6 17.3 %copy-start.29 = (bf16[1,128,768]{1,2,0:T(8,128)(2,1)}, bf16[1,128,768]{1,2,0:T(8,128)(2,1)S(1)}, u32[]{:S(2)}) copy-start(bf16[1,128,768]{1,2,0:T(8,128)(2,1)S(1)} %copy.268) | copy-start | bytes 589828
  340.6 19.3 %copy-start.58 = (f32[768]{0:T(1024)S(1)}, f32[768]{0:T(1024)}, u32[]{:S(2)}) copy-start(f32[768]{0:T(1024)} %get-tuple-element.102) | copy-start | bytes 9220
  356.9 1.6 copy-start.1
  356.9 2.2 copy-start.21
  356.9 85.8 %copy-start.3 = (bf16[1,768,768]{2,0,1:T(2,128)(2,1)}, bf16[1,768,768]{2,0,1:T(2,128)(2,1)S(1)}, u32[]{:S(2)}) copy-start(bf16[1,768,768]{2,0,1:T(2,128)(2,1)S(1)} %get-tuple-element.123) | copy-start | bytes 3538948
  357.1 1.7 copy-start.25
  358.9 1.0 copy-start.6
  358.9 1.0 copy-start.64
  360.5 48.2 %copy-start.16 = (bf16[128,768]{0,1:T(8,128)(2,1)}, bf16[128,768]{0,1:T(8,128)(2,1)S(1)}, u32[]{:S(2)}) copy-start(bf16[128,768]{0,1:T(8,128)(2,1)S(1)} %copy.277) | copy-start | bytes 589828
  430.6 12.0 %copy-start.50 = (f32[12,128]{1,0:T(8,128)}, f32[12,128]{1,0:T(8,128)S(1)}, u32[]{:S(2)}) copy-start(f32[12,128]{1,0:T(8,128)S(1)} %log_add_fusion) | copy-start | bytes 18436
  430.6 12.0 %copy-start.7 = (f32[128,768]{1,0:T(8,128)S(1)}, f32[128,768]{1,0:T(8,128)}, u32[]{:S(2)}) copy-start(f32[128,768]{1,0:T(8,128)} %copy-done.6) | copy-start | bytes 1179652
  443.3 7.2 copy-start.34
  450.6 3.7 copy-start.5
  454.1 4.0 copy-start.41
  454.1 4.0 copy-start.43
  454.1 4.8 copy-start.4
  454.3 6.9 copy-start.51
  506.4 13.7 %copy-start.17 = (bf16[128,768]{0,1:T(8,128)(2,1)S(1)}, bf16[128,768]{0,1:T(8,128)(2,1)}, u32[]{:S(2)}) copy-start(bf16[128,768]{0,1:T(8,128)(2,1)} %copy-done.16) | copy-start | bytes 589828
  520.1 5.2 copy-start
  567.8 168.2 %all-to-all-start.1 = ((bf16[2,1,3072,768]{3,0,1,2:T(2,128)(2,1)}), bf16[2,1,3072,768]{3,0,1,2:T(2,128)(2,1)}, u32[]{:S(2)}, u32[]{:S(2)}) async-start(bf16[2,1,3072,768]{3,0,1,2:T(2,128)(2,1)} %pad_maximum_fusion), calls=%async_computation.1 | async-start | bytes 18874368 | tf_op jit(solution)/shard_map/all_to_all | solution.py:184
  572.7 9.4 copy-start.59
  572.7 9.4 copy-start.65
  572.7 544.7 %all-reduce.3.cloned.1.call-start = ((), (), s32[]{:S(2)}) async-start(), calls=%async_computation.5 | async-start | bytes 75497472 | tf_op jit(solution)/shard_map/psum | solution.py:212
  572.7 9.3 copy-start.8
  572.8 9.3 copy-start.22
  572.8 10.0 copy-start.13
  572.8 11.0 copy-start.2
  582.7 13.7 %copy-start.20 = (bf16[1,128,768]{2,1,0:T(8,128)(2,1)S(1)}, bf16[1,128,768]{2,1,0:T(8,128)(2,1)}, u32[]{:S(2)}) copy-start(bf16[1,128,768]{2,1,0:T(8,128)(2,1)} %param.16) | copy-start | bytes 589828
  582.7 13.7 %copy-start.57 = (f32[768]{0:T(1024)S(1)}, f32[768]{0:T(1024)}, u32[]{:S(2)}) copy-start(f32[768]{0:T(1024)} %copy-done.56) | copy-start | bytes 9220
  582.7 13.7 %copy-start.63 = (f32[128]{0:T(128)S(1)}, f32[128]{0:T(128)}, u32[]{:S(2)}) copy-start(f32[128]{0:T(128)} %copy-done.62) | copy-start | bytes 1540
  594.2 1.6 copy-start.37
  601.4 11.1 copy-start.11
  601.4 11.1 copy-start.26
  612.5 3.5 copy-start.9
  612.5 3.5 copy-start.31
  612.9 6.6 copy-start.14
  612.9 6.6 copy-start.33
  616.5 6.5 copy-start.42
  616.5 6.5 copy-start.44
  629.4 19.5 %copy-start.35 = (bf16[1,128,768]{2,1,0:T(8,128)(2,1)S(1)}, bf16[1,128,768]{2,1,0:T(8,128)(2,1)}, u32[]{:S(2)}) copy-start(bf16[1,128,768]{2,1,0:T(8,128)(2,1)} %param.19) | copy-start | bytes 589828
  814.4 77.0 %copy-start.61 = (f32[3,6]{1,0:T(4,128)S(1)}, f32[3,6]{1,0:T(4,128)}, u32[]{:S(2)}) copy-start(f32[3,6]{1,0:T(4,128)} %param.23) | copy-start | bytes 220
  814.4 77.0 %copy-start.66 = (f32[3,6]{1,0:T(4,128)S(1)}, f32[3,6]{1,0:T(4,128)}, u32[]{:S(2)}) copy-start(f32[3,6]{1,0:T(4,128)} %param.27) | copy-start | bytes 220
  814.4 77.0 %copy-start.67 = (f32[3,6]{1,0:T(4,128)S(1)}, f32[3,6]{1,0:T(4,128)}, u32[]{:S(2)}) copy-start(f32[3,6]{1,0:T(4,128)} %param.31) | copy-start | bytes 220
  891.4 6.9 copy-start.24
  898.3 219.1 %copy-start.40 = (f32[8,6,768]{2,0,1:T(8,128)S(1)}, f32[8,6,768]{2,0,1:T(8,128)}, u32[]{:S(2)}) copy-start(f32[8,6,768]{2,0,1:T(8,128)} %param.20) | copy-start | bytes 442372
  898.3 219.1 %copy-start.48 = (f32[8,6,768]{2,0,1:T(8,128)S(1)}, f32[8,6,768]{2,0,1:T(8,128)}, u32[]{:S(2)}) copy-start(f32[8,6,768]{2,0,1:T(8,128)} %param.24) | copy-start | bytes 442372
  898.3 219.1 %copy-start.49 = (f32[8,6,768]{2,0,1:T(8,128)S(1)}, f32[8,6,768]{2,0,1:T(8,128)}, u32[]{:S(2)}) copy-start(f32[8,6,768]{2,0,1:T(8,128)} %param.28) | copy-start | bytes 442372
  898.4 220.8 %copy-start.45 = (f32[2,6,2048]{2,0,1:T(2,128)S(1)}, f32[2,6,2048]{2,0,1:T(2,128)}, u32[]{:S(2)}) copy-start(f32[2,6,2048]{2,0,1:T(2,128)} %param.21) | copy-start | bytes 294916
  898.4 220.8 %copy-start.52 = (f32[2,6,2048]{2,0,1:T(2,128)S(1)}, f32[2,6,2048]{2,0,1:T(2,128)}, u32[]{:S(2)}) copy-start(f32[2,6,2048]{2,0,1:T(2,128)} %param.25) | copy-start | bytes 294916
  898.4 220.8 %copy-start.53 = (f32[2,6,2048]{2,0,1:T(2,128)S(1)}, f32[2,6,2048]{2,0,1:T(2,128)}, u32[]{:S(2)}) copy-start(f32[2,6,2048]{2,0,1:T(2,128)} %param.29) | copy-start | bytes 294916
  898.4 222.8 %copy-start.47 = (f32[16,768]{1,0:T(8,128)S(1)}, f32[16,768]{1,0:T(8,128)}, u32[]{:S(2)}) copy-start(f32[16,768]{1,0:T(8,128)} %param.22) | copy-start | bytes 147460
  898.4 222.7 %copy-start.54 = (f32[16,768]{1,0:T(8,128)S(1)}, f32[16,768]{1,0:T(8,128)}, u32[]{:S(2)}) copy-start(f32[16,768]{1,0:T(8,128)} %param.26) | copy-start | bytes 147460
  898.4 222.7 %copy-start.55 = (f32[16,768]{1,0:T(8,128)S(1)}, f32[16,768]{1,0:T(8,128)}, u32[]{:S(2)}) copy-start(f32[16,768]{1,0:T(8,128)} %param.30) | copy-start | bytes 147460
  (10 other events, 7.6 us)
Sparse Core Ops, SparseCore 0:
  11.6 73.3 all-gather.4
  88.6 189.2 all-gather.6
  281.5 77.8 all-gather.8
  814.5 302.8 all-reduce.2
where the time goes:
time: 1140 us; the launch traced here: 1130 us
  waiting for transfers between devices  364 us (32%)
  blocking collectives  283 us (25%)
  local copies, waits for them, and re-layouts  249 us (22%)
  matrix products  149 us (13%)
  other arithmetic  58.8 us (5%)
  between operations  15.8 us (1%)
    all_gather x1, blocking collectives, body(): lax.all_gather(gain_master.astype(jnp.bfloat16), ('dp', 'seq'), axis=1, t...  211 us
    psum x1, waiting for transfers between devices, body(): summed = lax.psum((g_attn, g_up, g_down, g_gain), ('dp', 'seq'))  206 us
    all_to_all x1, waiting for transfers between devices, body(): lax.all_to_all(kv_grad, 'seq', split_axis=2, concat_axis=1, tiled=True)  83.4 us
    all_gather x1, waiting for transfers between devices, body(): lax.all_gather(attn_master.astype(jnp.bfloat16), ('dp', 'seq'), axis=1, t...  74.5 us
    psum x1, blocking collectives, body(): summed = lax.psum((g_attn, g_up, g_down, g_gain), ('dp', 'seq'))  71.4 us
    concatenate x1, local copies, waits for them, and re-layouts, body(): jnp.concatenate([g_self_qkv, g_self_out[None], g_cross_query[None], g_cro...  48.4 us
    another operation x2, local copies, waits for them, and re-layouts, body(): jnp.stack([dk_two.reshape(examples, -1, width), dv_two.reshape(examples,...  40.8 us
  transfers between devices with their start and end apart: 6, of which 3 were waited for; matrix products, arithmetic and copies ran while one was open for 22% of the time, Pallas kernels for 0%

commit v1 on v0

--- a/solution.py
+++ b/solution.py
@@ -1,6 +1,9 @@
+import functools
 import jax
 import jax.numpy as jnp
 from jax import lax
+from jax.experimental import pallas as pl
+from jax.experimental.pallas import tpu as pltpu
 from jax.sharding import PartitionSpec as P
 
 H = 12
@@ -99,6 +102,425 @@
         first_new / fix_one / (jnp.sqrt(second_new / fix_two) + adam_eps) + decay_rate * master
     )
     return (master_new, first_new, second_new, master_new.astype(jnp.bfloat16))
+
+
+MESH = pl.DeviceIdType.MESH
+BF, F32 = jnp.bfloat16, jnp.float32
+ALL = slice(None)
+PARTS = (("A", 0, "xyz"), ("A", 1, "yzx"), ("A", 2, "zxy"), ("B", 0, "xyz"), ("B", 1, "yzx"), ("C", 0, "zxy"))
+
+def where_am_i():
+    dp, sq = lax.axis_index("dp"), lax.axis_index("seq")
+    return {"x": sq // 4, "y": sq % 4, "z": dp // 2, "c": dp % 2}
+
+def dev(at):
+    return (at["z"] * 2 + at["c"], at["x"] * 4 + at["y"])
+
+def moved(at, axis, step):
+    return {**at, axis: (at[axis] + step + 4) % 4}
+
+def gather_kernel(attn, wi, wo, info, A, B, C, infos, stage, recv, blk, blkA, blkB, blkC, irecv,
+                  ss, rs, sib_s, sib_r, as_, ar_, is_, ir_, ds_, dr_, own_s):
+    me = where_am_i()
+    dp, sq = lax.axis_index("dp"), lax.axis_index("seq")
+    bar = pltpu.get_barrier_semaphore()
+    for i in range(1, 16):
+        pl.semaphore_signal(bar, inc=1, device_id=(dp, (sq + i) % 16), device_id_type=MESH)
+    for i in range(1, 8):
+        pl.semaphore_signal(bar, inc=1, device_id=((dp + i) % 8, sq), device_id_type=MESH)
+    stage[:, 6:8, :] = jnp.zeros((16, 2, 640), F32)
+    for s in range(16):
+        stage[s, 0:6, 0:384] = attn[s // 2, :, 384 * (s % 2):384 * (s % 2) + 384]
+        stage[s, 0:6, 384:640] = wi[s // 8, :, 256 * (s % 8):256 * (s % 8) + 256]
+    pl.semaphore_wait(bar, 22)
+    def a2a(i):
+        peer = (sq + i) % 16
+        return pltpu.make_async_remote_copy(stage.at[peer], recv.at[sq], as_.at[i], ar_.at[i], device_id=(dp, peer), device_id_type=MESH)
+    def inf(i):
+        peer = (sq + i) % 16
+        return pltpu.make_async_remote_copy(info, irecv.at[sq], is_.at[i], ir_.at[i], device_id=(dp, peer), device_id_type=MESH)
+    for i in range(1, 16):
+        a2a(i).start()
+    for i in range(1, 16):
+        inf(i).start()
+    recv[sq] = stage[sq]
+    irecv[sq] = info[...]
+    blkC[...] = wo[...].astype(BF)
+    for i in range(1, 16):
+        a2a(i).wait_recv()
+    for k in range(16):
+        blk[6 * k:6 * k + 6, :] = recv[k, 0:6, :]
+    for p in range(3):
+        blkA[p] = blk[32 * p:32 * p + 32, 0:384].astype(BF)
+    for p in range(2):
+        blkB[p] = blk[48 * p:48 * p + 48, 384:640].astype(BF)
+
+    def view(part, at):
+        name, p, _ = part
+        if name == "A":
+            return A.at[at["x"], at["y"], at["z"], at["c"], p]
+        if name == "B":
+            return B.at[at["x"], at["y"], at["z"], at["c"], p]
+        return C.at[at["z"], at["c"], at["x"], at["y"]]
+
+    def mine(part):
+        name, p, _ = part
+        return blkA.at[p] if name == "A" else blkB.at[p] if name == "B" else blkC
+
+    def group(part, t, step, half=None):
+        order = part[2]
+        at = moved(me, order[t], step)
+        for j in range(t):
+            at = {**at, order[j]: ALL}
+        if half is not None and t:
+            at = {**at, order[0]: pl.ds(2 * half, 2)}
+        return at
+
+    def send(n, t, kind):
+        part = PARTS[n]
+        axis = part[2][t]
+        step = 1 if kind in (0, 2) else -1
+        if kind < 2:
+            dst = view(part, group(part, t, 0))
+            src = mine(part) if t == 0 else dst
+        else:
+            dst = src = view(part, group(part, t, -step, kind - 2))
+        return pltpu.make_async_remote_copy(src, dst, ss.at[n, t, kind], rs.at[n, t, kind], device_id=dev(moved(me, axis, step)), device_id_type=MESH)
+
+    def arrival(n, t, kind):
+        part = PARTS[n]
+        axis = part[2][t]
+        step = 1 if kind in (0, 2) else -1
+        if kind < 2:
+            dst = view(part, group(part, t, -step))
+        else:
+            dst = view(part, group(part, t, -2 * step, kind - 2))
+        return pltpu.make_async_remote_copy(dst, dst, ss.at[n, t, kind], rs.at[n, t, kind], device_id=dev(moved(me, axis, step)), device_id_type=MESH)
+
+    def kinds(n, t):
+        return (0, 1, 2, 3) if t else (0, 1, 2 + n % 2)
+
+    def sibling(n, j, c):
+        part = PARTS[n]
+        steps = (0, -1, 1, 2)
+        at = {**group(part, 2, steps[j]), "c": c}
+        v = view(part, at)
+        return pltpu.make_async_remote_copy(v, v, sib_s.at[n, j], sib_r.at[n, j], device_id=dev({**me, "c": 1 - me["c"]}), device_id_type=MESH)
+
+    owns = [pltpu.make_async_copy(mine(PARTS[n]), view(PARTS[n], me), own_s.at[n]) for n in range(6)]
+    for o in owns:
+        o.start()
+    for t in range(3):
+        for n in range(6):
+            if t == 1:
+                owns[n].wait()
+            if t:
+                for k in kinds(n, t - 1)[2:]:
+                    arrival(n, t - 1, k).wait_recv()
+            send(n, t, 0).start()
+            send(n, t, 1).start()
+            if t == 2:
+                sibling(n, 0, me["c"]).start()
+        for n in range(6):
+            for k in (0, 1):
+                arrival(n, t, k).wait_recv()
+                if 2 + k in kinds(n, t):
+                    send(n, t, 2 + k).start()
+                if t == 2:
+                    sibling(n, 1 + k, me["c"]).start()
+    for i in range(1, 16):
+        inf(i).wait_recv()
+    tile = jnp.sum(irecv[...], axis=0)
+    infos[dp] = tile
+    def dpx(i):
+        return pltpu.make_async_remote_copy(infos.at[dp], infos.at[dp], ds_.at[i], dr_.at[i], device_id=((dp + i) % 8, sq), device_id_type=MESH)
+    def dpx_in(i):
+        return pltpu.make_async_remote_copy(infos.at[(dp - i + 8) % 8], infos.at[(dp - i + 8) % 8], ds_.at[i], dr_.at[i], device_id=((dp + i) % 8, sq), device_id_type=MESH)
+    for i in range(1, 8):
+        dpx(i).start()
+    for n in range(6):
+        for k in (2, 3):
+            arrival(n, 2, k).wait_recv()
+        sibling(n, 3, me["c"]).start()
+    for i in range(1, 8):
+        dpx_in(i).wait_recv()
+    for n in range(6):
+        for j in range(4):
+            sibling(n, j, 1 - me["c"]).wait_recv()
+    for i in range(1, 16):
+        a2a(i).wait_send()
+        inf(i).wait_send()
+    for i in range(1, 8):
+        dpx(i).wait_send()
+    for n in range(6):
+        for t in range(3):
+            for k in kinds(n, t):
+                send(n, t, k).wait_send()
+        for j in range(4):
+            sibling(n, j, me["c"]).wait_send()
+
+def gather(attn, wi, wo, info):
+    V = pl.BlockSpec(memory_space=pltpu.VMEM)
+    H = pl.BlockSpec(memory_space=pl.ANY)
+    D = pltpu.SemaphoreType.DMA
+    return pl.pallas_call(
+        gather_kernel,
+        out_shape=(jax.ShapeDtypeStruct((4, 4, 4, 2, 3, 32, 384), BF),
+                   jax.ShapeDtypeStruct((4, 4, 4, 2, 2, 48, 256), BF),
+                   jax.ShapeDtypeStruct((4, 2, 4, 4, 16, 768), BF),
+                   jax.ShapeDtypeStruct((8, 8, 128), F32)),
+        in_specs=[V] * 4, out_specs=(H, H, H, V),
+        scratch_shapes=[pltpu.VMEM((16, 8, 640), F32), pltpu.VMEM((16, 8, 640), F32), pltpu.VMEM((96, 640), F32),
+                        pltpu.VMEM((3, 32, 384), BF), pltpu.VMEM((2, 48, 256), BF), pltpu.VMEM((16, 768), BF),
+                        pltpu.VMEM((16, 8, 128), F32),
+                        D((6, 3, 4)), D((6, 3, 4)), D((6, 4)), D((6, 4)), D((16,)), D((16,)), D((16,)), D((16,)), D((8,)), D((8,)), D((6,))],
+        compiler_params=pltpu.CompilerParams(collective_id=0, has_side_effects=True, vmem_limit_bytes=32 << 20),
+        name="gather_weights",
+    )(attn, wi, wo, info)
+
+def info_tile(gain, mem_len):
+    sq = lax.axis_index("seq")
+    t = jnp.zeros((8, 128), F32)
+    t = lax.dynamic_update_slice(t, gain.astype(BF).astype(F32), (0, 6 * sq))
+    return lax.dynamic_update_slice(t, mem_len.astype(F32)[:, None], (3, sq))
+
+def scatter_kernel(GA, GB, GC, gg, oA, oB, oC, oG, accA, accB, accC, sibA, sibB, sibC,
+                   hA2, hB2, hC2, fA2, fB2, fC2, hA1, hB1, hC1, fA1, fB1, fC1, hA0, hB0, hC0, fA0, fB0, fC0,
+                   blk, stage, recv, gdp, gsum, gsq,
+                   ss, rs, sib_s, sib_r, loc_s, as_, ar_, is_, ir_, ds_, dr_):
+    me = where_am_i()
+    dp, sq = lax.axis_index("dp"), lax.axis_index("seq")
+    acc = {"A": accA, "B": accB, "C": accC}
+    sib = {"A": sibA, "B": sibB, "C": sibC}
+    hop = {2: {"A": hA2, "B": hB2, "C": hC2}, 1: {"A": hA1, "B": hB1, "C": hC1}, 0: {"A": hA0, "B": hB0, "C": hC0}}
+    fin = {2: {"A": fA2, "B": fB2, "C": fC2}, 1: {"A": fA1, "B": fB1, "C": fC1}, 0: {"A": fA0, "B": fB0, "C": fC0}}
+    bar = pltpu.get_barrier_semaphore()
+    for i in range(1, 16):
+        pl.semaphore_signal(bar, inc=1, device_id=(dp, (sq + i) % 16), device_id_type=MESH)
+    for i in range(1, 8):
+        pl.semaphore_signal(bar, inc=1, device_id=((dp + i) % 8, sq), device_id_type=MESH)
+    pl.semaphore_wait(bar, 22)
+
+    def idx(part, at):
+        name, p, _ = part
+        if name == "C":
+            return (at["z"], at["x"], at["y"])
+        return (p, at["x"], at["y"], at["z"])
+
+    def source(part, at, c):
+        name, p, _ = part
+        if name == "A":
+            return GA.at[at["x"], at["y"], at["z"], c, p]
+        if name == "B":
+            return GB.at[at["x"], at["y"], at["z"], c, p]
+        return GC.at[at["z"], c, at["x"], at["y"]]
+
+    def names(part):
+        return "zxy" if part[0] == "C" else "xyz"
+
+    def group(part, t, step):
+        order = part[2]
+        at = moved(me, order[t], step)
+        for j in range(t):
+            at = {**at, order[j]: ALL}
+        return at
+
+    def halved(part, t, at, half):
+        if t == 0:
+            return at
+        first = [a for a in names(part) if a in part[2][:t]][0]
+        return {**at, first: pl.ds(2 * half, 2)}
+
+    def done(part, t):
+        return [a for a in names(part) if a in part[2][:t]]
+
+    STEPS = (2, -1, 1, 0)
+    other = dev({**me, "c": 1 - me["c"]})
+
+    def sib_copy(n, j):
+        part = PARTS[n]
+        at = group(part, 2, STEPS[j])
+        return pltpu.make_async_remote_copy(source(part, at, 1 - me["c"]), sib[part[0]].at[idx(part, at)], sib_s.at[n, j], sib_r.at[n, j], device_id=other, device_id_type=MESH)
+
+    def loc_copy(n, j):
+        part = PARTS[n]
+        at = group(part, 2, STEPS[j])
+        return pltpu.make_async_copy(source(part, at, me["c"]), acc[part[0]].at[idx(part, at)], loc_s.at[n, j])
+
+    def slot(part):
+        return () if part[0] == "C" else (part[1],)
+
+    def kinds(n, t):
+        return (0, 1) if t else (n % 2,)
+
+    def hop_send(n, t, kind):
+        part = PARTS[n]
+        step = 1 if kind == 0 else -1
+        at = halved(part, t, group(part, t, 2 * step), kind)
+        return pltpu.make_async_remote_copy(acc[part[0]].at[idx(part, at)], hop[t][part[0]].at[slot(part) + (kind,)],
+                                            ss.at[n, t, kind], rs.at[n, t, kind], device_id=dev(moved(me, part[2][t], step)), device_id_type=MESH)
+
+    def fin_send(n, t, kind):
+        part = PARTS[n]
+        step = 1 if kind == 0 else -1
+        at = group(part, t, step)
+        return pltpu.make_async_remote_copy(acc[part[0]].at[idx(part, at)], fin[t][part[0]].at[slot(part) + (kind,)],
+                                            ss.at[n, t, 2 + kind], rs.at[n, t, 2 + kind], device_id=dev(moved(me, part[2][t], step)), device_id_type=MESH)
+
+    def each(part, t, at, fn, half=None):
+        axes = done(part, t)
+        sizes = [4] * len(axes)
+        offs = [0] * len(axes)
+        if half is not None and axes:
+            sizes[0] = 2
+            offs[0] = 2 * half
+        total = 1
+        for s in sizes:
+            total *= s
+        def one(i):
+            pos = []
+            rest = i
+            for s in sizes[::-1]:
+                pos.append(rest % s)
+                rest = rest // s
+            pos = pos[::-1]
+            where = dict(at)
+            for a, p, o in zip(axes, pos, offs):
+                where[a] = p + o
+            fn(idx(part, where), tuple(pos))
+        if total == 1:
+            one(0)
+        else:
+            pl.loop(0, total)(one)
+
+    def merge_sibling(n, j):
+        part = PARTS[n]
+        sib_copy(n, j).wait_recv()
+        loc_copy(n, j).wait()
+        a, b = acc[part[0]], sib[part[0]]
+        def fn(i, _):
+            a[i] = (a[i].astype(F32) + b[i].astype(F32)).astype(BF)
+        each(part, 2, group(part, 2, STEPS[j]), fn)
+
+    for j in range(4):
+        for n in range(6):
+            sib_copy(n, j).start()
+            loc_copy(n, j).start()
+    def dpx(i):
+        peer = (dp + i) % 8
+        return pltpu.make_async_remote_copy(gg.at[peer], gdp.at[dp], ds_.at[i], dr_.at[i], device_id=(peer, sq), device_id_type=MESH)
+    for i in range(1, 8):
+        dpx(i).start()
+    gdp[dp] = gg[dp]
+    for t in (2, 1, 0):
+        for n in range(6):
+            if t == 2:
+                merge_sibling(n, 0)
+            else:
+                finish(n, t + 1)
+            for k in kinds(n, t):
+                hop_send(n, t, k).start()
+        if t == 2:
+            for n in range(6):
+                merge_sibling(n, 1)
+                merge_sibling(n, 2)
+        for n in range(6):
+            part = PARTS[n]
+            for k in (0, 1):
+                if k in kinds(n, t):
+                    hop_send(n, t, k).wait_recv()
+                    a, b = acc[part[0]], hop[t][part[0]]
+                    def fn(i, pos, a=a, b=b, part=part, k=k):
+                        j = slot(part) + (k,) + pos
+                        a[i] = (a[i].astype(F32) + b[j].astype(F32)).astype(BF)
+                    each(part, t, group(part, t, 1 if k == 0 else -1), fn, k)
+                fin_send(n, t, k).start()
+        if t == 2:
+            for n in range(6):
+                merge_sibling(n, 3)
+
+        def finish(n, t):
+            part = PARTS[n]
+            fin_send(n, t, 0).wait_recv()
+            fin_send(n, t, 1).wait_recv()
+            a, b = acc[part[0]], fin[t][part[0]]
+            def fn(i, pos):
+                s = slot(part)
+                a[i] = (a[i].astype(F32) + b[s + (0,) + pos].astype(F32) + b[s + (1,) + pos].astype(F32)).astype(BF)
+            each(part, t, group(part, t, 0), fn)
+
+    for n in range(6):
+        part = PARTS[n]
+        fin_send(n, 0, 0).wait_recv()
+        fin_send(n, 0, 1).wait_recv()
+        a, b = acc[part[0]], fin[0][part[0]]
+        s = slot(part)
+        v = a[idx(part, me)].astype(F32) + b[s + (0,)].astype(F32) + b[s + (1,)].astype(F32)
+        if part[0] == "A":
+            blk[32 * part[1]:32 * part[1] + 32, 0:384] = v
+        elif part[0] == "B":
+            blk[48 * part[1]:48 * part[1] + 48, 384:640] = v
+        else:
+            oC[...] = v
+    stage[:, 6:8, :] = jnp.zeros((16, 2, 640), F32)
+    for k in range(16):
+        stage[k, 0:6, :] = blk[6 * k:6 * k + 6, :]
+    def a2a(i):
+        peer = (sq + i) % 16
+        return pltpu.make_async_remote_copy(stage.at[peer], recv.at[sq], as_.at[i], ar_.at[i], device_id=(dp, peer), device_id_type=MESH)
+    for i in range(1, 16):
+        a2a(i).start()
+    recv[sq] = stage[sq]
+    for i in range(1, 8):
+        dpx(i).wait_recv()
+    gsum[...] = jnp.sum(gdp[...], axis=0)
+    def inf(i):
+        peer = (sq + i) % 16
+        return pltpu.make_async_remote_copy(gsum, gsq.at[sq], is_.at[i], ir_.at[i], device_id=(dp, peer), device_id_type=MESH)
+    for i in range(1, 16):
+        inf(i).start()
+    gsq[sq] = gsum[...]
+    for i in range(1, 16):
+        a2a(i).wait_recv()
+    for s in range(16):
+        oA[s // 2, :, 384 * (s % 2):384 * (s % 2) + 384] = recv[s, 0:6, 0:384]
+        oB[s // 8, :, 256 * (s % 8):256 * (s % 8) + 256] = recv[s, 0:6, 384:640]
+    for i in range(1, 16):
+        inf(i).wait_recv()
+    oG[...] = jnp.sum(gsq[...], axis=0)
+    for i in range(1, 8):
+        dpx(i).wait_send()
+    for i in range(1, 16):
+        a2a(i).wait_send()
+        inf(i).wait_send()
+    for n in range(6):
+        for j in range(4):
+            sib_copy(n, j).wait_send()
+        for t in range(3):
+            for k in kinds(n, t):
+                hop_send(n, t, k).wait_send()
+            fin_send(n, t, 0).wait_send()
+            fin_send(n, t, 1).wait_send()
+
+def scatter(GA, GB, GC, gg):
+    V = pl.BlockSpec(memory_space=pltpu.VMEM)
+    H = pl.BlockSpec(memory_space=pl.ANY)
+    D = pltpu.SemaphoreType.DMA
+    bA, bB, bC = (32, 384), (48, 256), (16, 768)
+    M = lambda *s: pltpu.VMEM(s, BF)
+    trip = lambda pre: [M(3, *pre, *bA), M(2, *pre, *bB), M(*pre, *bC)]
+    return pl.pallas_call(
+        scatter_kernel,
+        out_shape=(jax.ShapeDtypeStruct((8, 6, 768), F32), jax.ShapeDtypeStruct((2, 6, 2048), F32),
+                   jax.ShapeDtypeStruct((16, 768), F32), jax.ShapeDtypeStruct((8, 128), F32)),
+        in_specs=[H] * 3 + [V], out_specs=(V,) * 4,
+        scratch_shapes=trip((4, 4, 4)) + trip((4, 4, 4)) + trip((2, 2, 4)) + trip((2, 4, 4)) + trip((2, 2)) + trip((2, 4)) + trip((2,)) + trip((2,))
+        + [pltpu.VMEM((96, 640), F32), pltpu.VMEM((16, 8, 640), F32), pltpu.VMEM((16, 8, 640), F32),
+           pltpu.VMEM((8, 8, 128), F32), pltpu.VMEM((8, 128), F32), pltpu.VMEM((16, 8, 128), F32),
+           D((6, 3, 4)), D((6, 3, 4)), D((6, 4)), D((6, 4)), D((6, 4)), D((16,)), D((16,)), D((16,)), D((16,)), D((8,)), D((8,))],
+        compiler_params=pltpu.CompilerParams(collective_id=1, has_side_effects=True, vmem_limit_bytes=56 << 20),
+        name="scatter_grads",
+    )(GA, GB, GC, gg)
 
 
 def body(
@@ -119,13 +541,13 @@
     ffn_out_second,
     gain_second,
 ):
-    attn_w, in_w, out_w, gain_w = (
-        lax.all_gather(attn_master.astype(jnp.bfloat16), ("dp", "seq"), axis=1, tiled=True),
-        lax.all_gather(ffn_in_master.astype(jnp.bfloat16), ("dp", "seq"), axis=1, tiled=True),
-        lax.all_gather(ffn_out_master.astype(jnp.bfloat16), ("dp", "seq"), axis=0, tiled=True),
-        lax.all_gather(gain_master.astype(jnp.bfloat16), ("dp", "seq"), axis=1, tiled=True),
-    )
-    gains = gain_w.astype(jnp.float32)
+    gath_a, gath_b, gath_c, infos = gather(
+        attn_master, ffn_in_master, ffn_out_master, info_tile(gain_master, mem_len)
+    )
+    attn_w = gath_a.reshape(8, 2, 768, 384).transpose(0, 2, 1, 3).reshape(8, 768, 768)
+    in_w = gath_b.reshape(2, 8, 768, 256).transpose(0, 2, 1, 3).reshape(2, 768, 2048)
+    out_w = gath_c.reshape(2048, 768)
+    gains = infos[:, :3, :96].transpose(1, 0, 2).reshape(3, 768)
     examples, tgt_len, width = dec_input.shape
     total_rows = examples * tgt_len
 
@@ -209,18 +631,17 @@
         [g_self_qkv, g_self_out[None], g_cross_query[None], g_cross_kv, g_cross_out[None]], axis=0
     )
     g_gain = jnp.stack([gain_one, gain_two, gain_three])
-    summed = lax.psum((g_attn, g_up, g_down, g_gain), ("dp", "seq"))
-    owner = lax.axis_index(("dp", "seq"))
-    shares = (
-        lax.dynamic_slice_in_dim(summed[0], owner * attn_master.shape[1], attn_master.shape[1], 1),
-        lax.dynamic_slice_in_dim(
-            summed[1], owner * ffn_in_master.shape[1], ffn_in_master.shape[1], 1
-        ),
-        lax.dynamic_slice_in_dim(
-            summed[2], owner * ffn_out_master.shape[0], ffn_out_master.shape[0], 0
-        ),
-        lax.dynamic_slice_in_dim(summed[3], owner * gain_master.shape[1], gain_master.shape[1], 1),
-    )
+    low_a = g_attn.reshape(8, 768, 2, 384).transpose(0, 2, 1, 3).astype(jnp.bfloat16)
+    low_b = g_up.reshape(2, 768, 8, 256).transpose(0, 2, 1, 3).astype(jnp.bfloat16)
+    tile_g = jnp.pad(g_gain.reshape(3, 8, 96).transpose(1, 0, 2), ((0, 0), (0, 5), (0, 32)))
+    share_a, share_b, share_c, share_g = scatter(
+        low_a.reshape(4, 4, 4, 2, 3, 32, 384),
+        low_b.reshape(4, 4, 4, 2, 2, 48, 256),
+        g_down.astype(jnp.bfloat16).reshape(4, 2, 4, 4, 16, 768),
+        tile_g,
+    )
+    share_g = lax.dynamic_slice_in_dim(share_g[:3], 6 * lax.axis_index("seq"), 6, 1)
+    shares = (share_a, share_b, share_c, share_g)
     attn_res = adam_update(attn_master, attn_first, attn_second, shares[0], rate_matrix)
     in_res = adam_update(ffn_in_master, ffn_in_first, ffn_in_second, shares[1], rate_matrix)
     out_res = adam_update(ffn_out_master, ffn_out_first, ffn_out_second, shares[2], rate_matrix)

time: 1140 us -> 794 us (0.70)
  blocking collectives: 283 us -> 0 us
  waiting for transfers between devices: 364 us -> 226 us
  Pallas kernels: 0 us -> 130 us
  local copies, waits for them, and re-layouts: 249 us -> 201 us
  between operations: 15.8 us -> 2.27 us
    all_gather x1 -> x0, blocking collectives: 211 us -> none  [body(): lax.all_gather(gain_master.astype(jnp.bfloat16), ('dp', 'seq'), axis=1, t...]
    psum x1 -> x0, waiting for transfers between devices: 206 us -> none  [body(): summed = lax.psum((g_attn, g_up, g_down, g_gain), ('dp', 'seq'))]
    all_to_all x1, waiting for transfers between devices: 0.01 us -> 143 us  [body(): lax.all_to_all(local_pair, 'seq', split_axis=1, concat_axis=2, tiled=True)]
    pallas_call x0 -> x2, Pallas kernels: none -> 130 us  [the longest x1 69.9 us: scatter(): pl.pallas_call(scatter_kernel, out_shape=(jax.ShapeDtypeStruct((8, 6, 768...]
    all_gather x3 -> x0, waiting for transfers between devices: 74.6 us -> none  [the longest x1 74.5 us: body(): lax.all_gather(attn_master.astype(jnp.bfloat16), ('dp', 'seq'), axis=1, t...]
    psum x1 -> x0, blocking collectives: 71.4 us -> none  [body(): summed = lax.psum((g_attn, g_up, g_down, g_gain), ('dp', 'seq'))]
    concatenate x1 -> x2, local copies, waits for them, and re-layouts: 48.4 us -> 9.07 us  [body(): jnp.concatenate([g_self_qkv, g_self_out[None], g_cross_query[None], g_cro...]
    dot_general x3 -> x2, local copies, waits for them, and re-layouts: 38.8 us -> 3.48 us  [weight_grad(): jnp.einsum('rd,re->de', left, right, preferred_element_type=jnp.float32)]
  transfers between devices with their start and end apart: 6 -> 2, of which waited for: 3 -> 2; matrix products, arithmetic and copies ran while one was open for 22% -> 13% of each run, Pallas kernels for 0% -> 0%
where the time goes in v1:
time: 794 us; the launch traced here: 785 us
  waiting for transfers between devices  226 us (28%)
  local copies, waits for them, and re-layouts  201 us (25%)
  matrix products  147 us (19%)
  Pallas kernels  130 us (16%)
  other arithmetic  60.3 us (8%)
  starting transfers between devices  17.9 us (2%)
    all_to_all x1, waiting for transfers between devices, body(): lax.all_to_all(local_pair, 'seq', split_axis=1, concat_axis=2, tiled=True)  143 us
    all_to_all x1, waiting for transfers between devices, body(): lax.all_to_all(kv_grad, 'seq', split_axis=2, concat_axis=1, tiled=True)  82.1 us
    pallas_call x1, Pallas kernels, scatter(): pl.pallas_call(scatter_kernel, out_shape=(jax.ShapeDtypeStruct((8, 6, 768...  69.9 us
    pallas_call x1, Pallas kernels, gather(): pl.pallas_call(gather_kernel, out_shape=(jax.ShapeDtypeStruct((4, 4, 4, 2...  59.9 us
    another operation x2, local copies, waits for them, and re-layouts, body(): jnp.stack([dk_two.reshape(examples, -1, width), dv_two.reshape(examples,...  40.9 us
    unnamed x140, local copies, waits for them, and re-layouts  30.1 us
    another operation x1, other arithmetic, body(): jnp.stack([dk_two.reshape(examples, -1, width), dv_two.reshape(examples,...  22.3 us
    another operation x2, local copies, waits for them, and re-layouts  21.8 us
  transfers between devices with their start and end apart: 2, of which 2 were waited for; matrix products, arithmetic and copies ran while one was open for 13% of the time, Pallas kernels for 0%

profile of v1, /device:TPU:0, one launch (start us, length us, event | category | flops | bytes accessed | tf_op | source)
XLA Modules:
  0.0 784.6 jit_solution(14983373429846770813)
XLA Ops:
  5.1 59.9 %gather_weights.1 = (bf16[4,4,4,2,3,32,384]{6,5,4,3,2,1,0:T(8,128)(2,1)S(1)}, bf16[4,4,4,2,2,48,256]{6,5,4,3,2,1,0:T(8,128)(2,1)S(1)}, bf16[4,2,4,4,16,768]{5,4,3,2,1,0:T(8,128)(2,1)S(1)}, f32[8,8,128]{2,1,0:T(8,128)S(1)}) custom-call(f32[8,6,768]{2,1,0:T(8,128)S(1)} %copy.130.attn, f32[2,6,2048]{2,1,0:T(8,128)S(1)} %copy.131.wi, f32[16,768]{1,0:T(8,128)S(1)} %copy-done.2, ...), custom_call_target="tpu_custom_call" | custom-call | tf_op jit(solution)/shard_map/gather_weights/pallas_call | solution.py:266
  65.1 3.7 copy-done
  68.8 2.6 copy-done.1
  71.5 12.7 %copy.132 = bf16[8,2,768,384]{2,3,1,0:T(8,128)(2,1)} copy(bf16[8,2,768,384]{3,2,1,0:T(8,128)(2,1)} %bitcast.296) | data formatting | bytes 18874368 | tf_op jit(solution)/shard_map/reshape | solution.py:547
  84.2 1.8 slice.101
  87.3 12.0 %convert_bitcast_fusion = bf16[2,16,192,768]{3,2,1,0:T(8,128)(2,1)} fusion(bf16[2,768,768,1]{1,2,3,0:T(8,128)(2,1)S(1)} %bitcast.326, bf16[16,192,768]{2,1,0:T(8,128)(2,1)} %param.17), kind=kOutput, calls=%fused_computation.9 | convolution fusion | flops 7252475904 | bytes 16515072 | tf_op jit(solution)/shard_map/emd,kdf->kemf/dot_general | solution.py:572
  99.3 8.3 %copy.135 = bf16[2,16,192,768]{3,2,0,1:T(8,128)(2,1)} copy(bf16[2,16,192,768]{3,2,1,0:T(8,128)(2,1)} %convert_bitcast_fusion) | data formatting | bytes 18874368 | tf_op jit(solution)/shard_map/convert_element_type | solution.py:574
  107.6 5.3 all-to-all-start
  112.9 4.0 slice.95
  117.3 3.2 fusion.14
  122.0 3.3 fusion.107
  126.4 1.5 multiply_reduce_fusion.7
  129.7 1.8 copy.137
  131.4 6.3 copy.194
  138.4 143.4 %all-to-all-done = bf16[2,16,192,768]{3,2,0,1:T(8,128)(2,1)} async-done(((bf16[2,16,192,768]{3,2,0,1:T(8,128)(2,1)}), bf16[2,16,192,768]{3,2,0,1:T(8,128)(2,1)}, u32[]{:S(2)}, u32[]{:S(2)}) %all-to-all-start) | async-done | bytes 9437216 | tf_op jit(solution)/shard_map/all_to_all | solution.py:575
  281.8 8.4 %fusion.108 = (bf16[1,16,192,768]{3,2,0,1:T(8,128)(2,1)}, bf16[1,16,192,768]{3,2,0,1:T(8,128)(2,1)}) fusion(bf16[2,16,192,768]{3,2,0,1:T(8,128)(2,1)} %all-to-all-done), kind=kLoop, calls=%fused_computation.185 | loop fusion | bytes 18874368 | tf_op jit(solution)/shard_map/slice | solution.py:578
  290.2 9.1 %copy.136 = bf16[1,16,192,768]{2,1,3,0:T(8,128)(2,1)} copy(bf16[1,16,192,768]{3,2,0,1:T(8,128)(2,1)} %get-tuple-element.125) | data formatting | bytes 9437184 | tf_op jit(solution)/shard_map/slice | solution.py:579
  299.3 10.7 %reshape.401 = bf16[3072,12,64]{0,2,1:T(8,128)(2,1)} reshape(bf16[1,16,192,768]{2,1,3,0:T(8,128)(2,1)} %copy.136) | data formatting | bytes 9437184 | tf_op jit(solution)/shard_map/reshape.53
  310.0 9.1 %copy.138 = bf16[1,16,192,768]{2,1,3,0:T(8,128)(2,1)} copy(bf16[1,16,192,768]{3,2,0,1:T(8,128)(2,1)} %get-tuple-element.124) | data formatting | bytes 9437184 | tf_op jit(solution)/shard_map/slice | solution.py:578
  319.1 11.2 %reshape.403 = bf16[3072,12,64]{0,2,1:T(8,128)(2,1)} reshape(bf16[1,16,192,768]{2,1,3,0:T(8,128)(2,1)} %copy.138) | data formatting | bytes 9437184 | tf_op jit(solution)/shard_map/reshape.49
  330.2 12.2 %fusion = (f32[12,128]{1,0:T(8,128)}, f32[12,128,3072]{2,1,0:T(8,128)}) fusion(pred[3072]{0:T(1024)(128)(4,1)S(1)} %iota_compare_fusion.1, bf16[128,12,64]{0,2,1:T(8,128)(2,1)} %bitcast.324, bf16[3072,12,64]{0,2,1:T(8,128)(2,1)} %reshape.403), kind=kOutput, calls=%fused_computation.5 | convolution fusion | flops 618134016 | bytes 23798784 | tf_op jit(solution)/shard_map/eqhc,ekhc->ehqk/dot_general | solution.py:55
  342.5 11.0 %exponential_reduce_fusion = f32[12,128]{1,0:T(8,128)} fusion(f32[12,128,3072]{2,1,0:T(8,128)} %get-tuple-element.136, f32[12,128]{1,0:T(8,128)} %get-tuple-element.135, pred[3072]{0:T(1024)(128)(4,1)S(1)} %iota_compare_fusion.1), kind=kLoop, calls=%fused_computation.3 | loop fusion | flops 18872832 | bytes 18889728 | tf_op jit(solution)/shard_map/reduce_sum | solution.py:64
  354.2 12.0 %convolution_convert_fusion.8 = bf16[12,64,128]{2,1,0:T(8,128)(2,1)S(1)} fusion(bf16[3072,12,64]{0,2,1:T(8,128)(2,1)} %reshape.401, f32[12,128,3072]{2,1,0:T(8,128)} %get-tuple-element.136, f32[12,128]{1,0:T(8,128)S(1)} %log_add_fusion, pred[3072]{0:T(1024)(128)(4,1)S(1)} %iota_compare_fusion.1), kind=kOutput, calls=%fused_computation.46 | convolution fusion | flops 622952448 | bytes 23798784 | tf_op jit(solution)/shard_map/ehqk,ekhc->eqhc/dot_general | solution.py:66
  366.9 5.0 convolution_bitcast_fusion.1
  375.7 2.9 multiply_reduce_fusion.2
  381.2 1.7 copy.142
  383.0 15.1 %multiply_reduce_fusion = (f32[12,128]{1,0:T(8,128)}, f32[12,128,3072]{2,1,0:T(8,128)}) fusion(f32[12,128,3072]{2,1,0:T(8,128)} %get-tuple-element.136, f32[12,128]{1,0:T(8,128)} %copy-done.43, pred[3072]{0:T(1024)(128)(4,1)S(1)} %iota_compare_fusion.1, bf16[128,12,64]{0,2,1:T(8,128)(2,1)} %bitcast.329, bf16[3072,12,64]{0,2,1:T(8,128)(2,1)} %reshape.401), kind=kOutput, calls=%fused_computation.1 | convolution fusion | flops 627571200 | bytes 42679296 | tf_op jit(solution)/shard_map/eqhc,ekhc->ehqk/dot_general | solution.py:78
  398.1 10.2 %convolution_convert_fusion = bf16[12,64,3072]{2,1,0:T(8,128)(2,1)} fusion(bf16[128,12,64]{0,2,1:T(8,128)(2,1)S(1)} %bitcast.330, f32[12,128,3072]{2,1,0:T(8,128)} %get-tuple-element.136, f32[12,128]{1,0:T(8,128)S(1)} %copy-done.44, pred[3072]{0:T(1024)(128)(4,1)S(1)} %iota_compare_fusion.1), kind=kOutput, calls=%fused_computation.10 | convolution fusion | flops 625213440 | bytes 23798784 | tf_op jit(solution)/shard_map/ehqk,eqhc->ekhc/dot_general | solution.py:72
  408.2 20.4 %copy.152 = bf16[1,1,3072,768]{3,0,1,2:T(2,128)(2,1)} copy(bf16[1,1,3072,768]{2,3,1,0:T(8,128)(2,1)} %bitcast.312) | data formatting | bytes 9437184 | tf_op jit(solution)/shard_map/stack;reshape | solution.py:605
  428.7 13.7 %multiply_convert_fusion = bf16[12,128,3072]{2,1,0:T(8,128)(2,1)S(1)} fusion(f32[12,128,3072]{2,1,0:T(8,128)} %get-tuple-element.141, f32[12,128,3072]{2,1,0:T(8,128)} %get-tuple-element.136, f32[12,128]{1,0:T(8,128)} %get-tuple-element.140, f32[12,128]{1,0:T(8,128)} %copy-done.43, pred[3072]{0:T(1024)(128)(4,1)S(1)} %iota_compare_fusion.1), kind=kLoop, calls=%fused_computation | loop fusion | flops 28311552 | bytes 47201280 | tf_op jit(solution)/shard_map/convert_element_type | solution.py:80
  442.4 3.6 multiply_convert_fusion.1
  446.0 1.6 copy-done.4
  447.6 20.5 %copy.151 = bf16[1,1,3072,768]{3,0,1,2:T(2,128)(2,1)} copy(bf16[1,1,3072,768]{2,3,1,0:T(8,128)(2,1)} %bitcast.307) | data formatting | bytes 9437184 | tf_op jit(solution)/shard_map/stack;reshape | solution.py:605
  468.0 22.3 %pad_maximum_fusion = bf16[2,1,3072,768]{3,0,1,2:T(2,128)(2,1)} fusion(bf16[1,1,3072,768]{3,0,1,2:T(2,128)(2,1)} %copy.152, bf16[1,1,3072,768]{3,0,1,2:T(2,128)(2,1)} %copy.151), kind=kLoop, calls=%fused_computation.7 | loop fusion | flops 18874368 | bytes 18874368 | tf_op jit(solution)/shard_map/stack | solution.py:605
  490.3 12.6 %all-to-all-start.1 = ((bf16[2,1,3072,768]{3,0,1,2:T(2,128)(2,1)}), bf16[2,1,3072,768]{3,0,1,2:T(2,128)(2,1)}, u32[]{:S(2)}, u32[]{:S(2)}) async-start(bf16[2,1,3072,768]{3,0,1,2:T(2,128)(2,1)} %pad_maximum_fusion), calls=%async_computation.1 | async-start | bytes 18874368 | tf_op jit(solution)/shard_map/all_to_all | solution.py:606
  503.0 8.6 %fusion.15 = bf16[12,64,128]{2,1,0:T(8,128)(2,1)S(1)} fusion(bf16[3072,12,64]{0,2,1:T(8,128)(2,1)} %reshape.403, bf16[12,128,3072]{2,1,0:T(8,128)(2,1)} %copy-done.4), kind=kOutput, calls=%fused_computation.45 | convolution fusion | flops 604176384 | bytes 14352384 | tf_op jit(solution)/shard_map/ehqk,ekhc->eqhc/dot_general | solution.py:82
  515.3 1.8 copy.143
  517.0 2.3 convolution_convert_fusion.9
  519.3 1.7 copy.149
  521.1 1.7 multiply_reduce_fusion.1
  524.8 2.0 fusion.18
  526.8 1.7 copy.148
  528.6 2.0 fusion.17
  530.6 1.7 copy.147
  532.3 4.2 convolution_convert_fusion.3
  536.5 6.0 copy.159
  542.5 1.7 copy.191
  544.2 1.8 copy.193
  546.0 5.9 convolution_convert_fusion.1
  551.9 9.0 %copy.161 = bf16[2,768,8,256]{3,1,2,0:T(8,128)(2,1)} copy(bf16[2,768,8,256]{1,3,2,0:T(8,128)(2,1)} %bitcast.308) | data formatting | bytes 12582912 | tf_op jit(solution)/shard_map/convert_element_type | solution.py:635
  562.4 4.2 fusion.60
  568.9 2.4 constant_dynamic-update-slice_fusion.1
  571.9 2.1 fusion.55
  574.0 1.6 fusion.8
  576.7 1.9 fusion.19
  580.1 2.7 convolution_convert_fusion.2
  582.7 82.1 %all-to-all-done.1 = bf16[2,1,3072,768]{3,0,1,2:T(2,128)(2,1)} async-done(((bf16[2,1,3072,768]{3,0,1,2:T(2,128)(2,1)}), bf16[2,1,3072,768]{3,0,1,2:T(2,128)(2,1)}, u32[]{:S(2)}, u32[]{:S(2)}) %all-to-all-start.1) | async-done | bytes 9437216 | tf_op jit(solution)/shard_map/all_to_all | solution.py:606
  664.8 8.5 %copy.153 = bf16[2,1,3072,768]{3,2,0,1:T(8,128)(2,1)} copy(bf16[2,1,3072,768]{3,0,1,2:T(2,128)(2,1)} %all-to-all-done.1) | data formatting | bytes 18874368 | tf_op jit(solution)/shard_map/all_to_all | solution.py:606
  673.4 12.4 %convolution_bitcast_fusion = f32[16,192,768]{2,1,0:T(8,128)} fusion(bf16[2,16,192,768]{3,2,1,0:T(8,128)(2,1)} %bitcast.322, bf16[2,768,768,1]{1,2,3,0:T(8,128)(2,1)S(1)} %bitcast.327), kind=kOutput, calls=%fused_computation.16 | convolution fusion | flops 7247757312 | bytes 21233664 | tf_op jit(solution)/shard_map/kemf,kdf->emd/dot_general | solution.py:608
  685.8 11.5 %bitcast_convert_fusion = bf16[2,768,768]{2,1,0:T(8,128)(2,1)} fusion(bf16[2,16,192,768]{3,2,1,0:T(8,128)(2,1)S(1)} %bitcast.323, bf16[16,192,768]{2,1,0:T(8,128)(2,1)} %param.17), kind=kOutput, calls=%fused_computation.11 | convolution fusion | flops 7248936960 | bytes 16515072 | tf_op jit(solution)/shard_map/emd,kemf->kdf/dot_general | solution.py:607
  697.3 3.0 copy.160
  700.3 1.7 constant_dynamic-update-slice_fusion
  702.0 1.5 fusion.12
  703.6 69.9 %scatter_grads.1 = (f32[8,6,768]{2,1,0:T(8,128)}, f32[2,6,2048]{2,1,0:T(8,128)}, f32[16,768]{1,0:T(8,128)}, f32[8,128]{1,0:T(8,128)}) custom-call(bf16[4,4,4,2,3,32,384]{6,5,4,3,2,1,0:T(8,128)(2,1)} %bitcast.313, bf16[4,4,4,2,2,48,256]{6,5,4,3,2,1,0:T(8,128)(2,1)} %bitcast.309, bf16[4,2,4,4,16,768]{5,4,3,2,1,0:T(8,128)(2,1)} %bitcast.315, f32[8,8,128]{2,1,0:T(8,128)} %pad.4.gg), custom_call_target="tpu_custom_call" | custom-call | tf_op jit(solution)/shard_map/scatter_grads/pallas_call | solution.py:512
  (181 shorter events, 41.6 us)
Async XLA Ops:
  4.3 0.8 copy-start.2
  65.1 3.7 copy-start
  68.8 2.6 copy-start.1
  86.0 1.4 copy-start.23
  107.6 9.5 %copy-start.17 = (bf16[1,128,768]{2,1,0:T(8,128)(2,1)S(1)}, bf16[1,128,768]{2,1,0:T(8,128)(2,1)}, u32[]{:S(2)}) copy-start(bf16[1,128,768]{2,1,0:T(8,128)(2,1)} %param.16) | copy-start | bytes 589828
  107.6 174.2 %all-to-all-start = ((bf16[2,16,192,768]{3,2,0,1:T(8,128)(2,1)}), bf16[2,16,192,768]{3,2,0,1:T(8,128)(2,1)}, u32[]{:S(2)}, u32[]{:S(2)}) async-start(bf16[2,16,192,768]{3,2,0,1:T(8,128)(2,1)} %copy.135), calls=%async_computation | async-start | bytes 18874368 | tf_op jit(solution)/shard_map/all_to_all | solution.py:575
  117.0 8.3 %copy-start.47 = (f32[768]{0:T(1024)}, f32[768]{0:T(1024)S(1)}, u32[]{:S(2)}) copy-start(f32[768]{0:T(1024)S(1)} %mul.487) | copy-start | bytes 9220
  117.2 3.6 copy-start.59
  120.5 0.7 copy-start.30
  120.5 0.8 copy-start.31
  120.8 0.9 copy-start.5
  122.0 5.9 copy-start.28
  125.4 1.0 copy-start.9
  125.4 2.6 copy-start.11
  354.2 12.0 %copy-start.43 = (f32[12,128]{1,0:T(8,128)}, f32[12,128]{1,0:T(8,128)S(1)}, u32[]{:S(2)}) copy-start(f32[12,128]{1,0:T(8,128)S(1)} %log_add_fusion) | copy-start | bytes 18436
  354.2 12.1 %copy-start.13 = (bf16[1,768,2,384]{1,3,2,0:T(8,128)(2,1)S(1)}, bf16[1,768,2,384]{1,3,2,0:T(8,128)(2,1)}, u32[]{:S(2)}) copy-start(bf16[1,768,2,384]{1,3,2,0:T(8,128)(2,1)} %get-tuple-element.121) | copy-start | bytes 3538948
  354.2 12.7 %copy-start.49 = (f32[768]{0:T(1024)S(1)}, f32[768]{0:T(1024)}, u32[]{:S(2)}) copy-start(f32[768]{0:T(1024)} %mul.501) | copy-start | bytes 9220
  366.2 8.5 %copy-start.32 = (bf16[12,64,128]{2,1,0:T(8,128)(2,1)}, bf16[12,64,128]{2,1,0:T(8,128)(2,1)S(1)}, u32[]{:S(2)}) copy-start(bf16[12,64,128]{2,1,0:T(8,128)(2,1)S(1)} %convolution_convert_fusion.8) | copy-start | bytes 589828
  366.2 7.1 copy-start.35
  366.9 11.7 %copy-start.14 = (f32[128,768]{1,0:T(8,128)}, f32[128,768]{1,0:T(8,128)S(1)}, u32[]{:S(2)}) copy-start(f32[128,768]{1,0:T(8,128)S(1)} %get-tuple-element.138) | copy-start | bytes 1179652
  366.9 11.7 %copy-start.58 = (f32[128]{0:T(128)}, f32[128]{0:T(128)S(1)}, u32[]{:S(2)}) copy-start(f32[128]{0:T(128)S(1)} %add_rsqrt_fusion) | copy-start | bytes 1540
  371.9 1.3 copy-start.7
  372.0 2.9 slice-start
  373.3 2.4 slice-start.1
  374.7 4.8 copy-start.38
  374.7 4.8 copy-start.39
  379.5 0.7 copy-start.20
  383.0 15.1 %copy-start.25 = (bf16[128,768]{0,1:T(8,128)(2,1)S(1)}, bf16[128,768]{0,1:T(8,128)(2,1)}, u32[]{:S(2)}) copy-start(bf16[128,768]{0,1:T(8,128)(2,1)} %copy.142) | copy-start | bytes 589828
  383.0 15.1 %copy-start.44 = (f32[12,128]{1,0:T(8,128)S(1)}, f32[12,128]{1,0:T(8,128)}, u32[]{:S(2)}) copy-start(f32[12,128]{1,0:T(8,128)} %copy-done.43) | copy-start | bytes 18436
  428.7 13.7 %copy-start.18 = (bf16[128,768]{0,1:T(8,128)(2,1)S(1)}, bf16[128,768]{0,1:T(8,128)(2,1)}, u32[]{:S(2)}) copy-start(bf16[128,768]{0,1:T(8,128)(2,1)} %copy.137) | copy-start | bytes 589828
  442.4 5.2 copy-start.4
  490.3 174.5 %all-to-all-start.1 = ((bf16[2,1,3072,768]{3,0,1,2:T(2,128)(2,1)}), bf16[2,1,3072,768]{3,0,1,2:T(2,128)(2,1)}, u32[]{:S(2)}, u32[]{:S(2)}) async-start(bf16[2,1,3072,768]{3,0,1,2:T(2,128)(2,1)} %pad_maximum_fusion), calls=%async_computation.1 | async-start | bytes 18874368 | tf_op jit(solution)/shard_map/all_to_all | solution.py:606
  503.0 8.7 %copy-start.12 = (bf16[1,768,2,384]{1,3,2,0:T(8,128)(2,1)S(1)}, bf16[1,768,2,384]{1,3,2,0:T(8,128)(2,1)}, u32[]{:S(2)}) copy-start(bf16[1,768,2,384]{1,3,2,0:T(8,128)(2,1)} %copy-done.11) | copy-start | bytes 3538948
  503.0 8.7 %copy-start.56 = (f32[128]{0:T(128)S(1)}, f32[128]{0:T(128)}, u32[]{:S(2)}) copy-start(f32[128]{0:T(128)} %copy-done.55) | copy-start | bytes 1540
  503.0 9.7 %copy-start.21 = (f32[128,768]{1,0:T(8,128)S(1)}, f32[128,768]{1,0:T(8,128)}, u32[]{:S(2)}) copy-start(f32[128,768]{1,0:T(8,128)} %copy-done.20) | copy-start | bytes 1179652
  503.0 11.3 %copy-start.10 = (bf16[1,768,2,384]{1,3,2,0:T(8,128)(2,1)S(1)}, bf16[1,768,2,384]{1,3,2,0:T(8,128)(2,1)}, u32[]{:S(2)}) copy-start(bf16[1,768,2,384]{1,3,2,0:T(8,128)(2,1)} %copy-done.9) | copy-start | bytes 3538948
  511.6 1.9 copy-start.26
  511.6 20.7 %copy-start.48 = (f32[768]{0:T(1024)S(1)}, f32[768]{0:T(1024)}, u32[]{:S(2)}) copy-start(f32[768]{0:T(1024)} %copy-done.47) | copy-start | bytes 9220
  513.5 0.7 copy-start.19
  524.1 0.7 copy-start.22
  524.8 21.2 %copy-start.50 = (f32[768]{0:T(1024)S(1)}, f32[768]{0:T(1024)}, u32[]{:S(2)}) copy-start(f32[768]{0:T(1024)} %mul.501) | copy-start | bytes 9220
  546.0 15.7 %copy-start.53 = (f32[768]{0:T(1024)S(1)}, f32[768]{0:T(1024)}, u32[]{:S(2)}) copy-start(f32[768]{0:T(1024)} %get-tuple-element.92) | copy-start | bytes 9220
  567.4 8.3 %copy-start.27 = (bf16[12,64,128]{2,1,0:T(8,128)(2,1)S(1)}, bf16[12,64,128]{2,1,0:T(8,128)(2,1)}, u32[]{:S(2)}) copy-start(bf16[12,64,128]{2,1,0:T(8,128)(2,1)} %copy-done.26) | copy-start | bytes 589828
  567.4 8.3 %copy-start.57 = (f32[128]{0:T(128)S(1)}, f32[128]{0:T(128)}, u32[]{:S(2)}) copy-start(f32[128]{0:T(128)} %copy-done.55) | copy-start | bytes 1540
  567.4 9.0 %copy-start.8 = (f32[2,128,2048]{1,2,0:T(8,128)S(1)}, f32[2,128,2048]{1,2,0:T(8,128)}, u32[]{:S(2)}) copy-start(f32[2,128,2048]{1,2,0:T(8,128)} %copy-done.7) | copy-start | bytes 6291460
  567.4 9.4 %copy-start.15 = (f32[128,768]{1,0:T(8,128)S(1)}, f32[128,768]{1,0:T(8,128)}, u32[]{:S(2)}) copy-start(f32[128,768]{1,0:T(8,128)} %copy-done.14) | copy-start | bytes 1179652
  567.4 12.7 %copy-start.36 = (bf16[1,128,768]{2,1,0:T(8,128)(2,1)S(1)}, bf16[1,128,768]{2,1,0:T(8,128)(2,1)}, u32[]{:S(2)}) copy-start(bf16[1,128,768]{2,1,0:T(8,128)(2,1)} %param.19) | copy-start | bytes 589828
  576.3 3.7 copy-start.6
  582.7 90.7 %copy-start.24 = (bf16[2,768,2,384]{1,3,2,0:T(8,128)(2,1)S(1)}, bf16[2,768,2,384]{1,3,2,0:T(8,128)(2,1)}, u32[]{:S(2)}) copy-start(bf16[2,768,2,384]{1,3,2,0:T(8,128)(2,1)} %copy-done.23) | copy-start | bytes 7077892
  673.4 12.4 %copy-start.16 = (bf16[2,1,3072,768]{3,2,0,1:T(8,128)(2,1)S(1)}, bf16[2,1,3072,768]{3,2,0,1:T(8,128)(2,1)}, u32[]{:S(2)}) copy-start(bf16[2,1,3072,768]{3,2,0,1:T(8,128)(2,1)} %copy.153) | copy-start | bytes 28311556
  697.3 4.8 copy-start.33
  697.3 4.8 copy-start.34
  703.5 70.0 %copy-start.37 = (f32[8,6,768]{2,0,1:T(8,128)S(1)}, f32[8,6,768]{2,0,1:T(8,128)}, u32[]{:S(2)}) copy-start(f32[8,6,768]{2,0,1:T(8,128)} %param.20) | copy-start | bytes 442372
  703.5 70.0 %copy-start.41 = (f32[8,6,768]{2,0,1:T(8,128)S(1)}, f32[8,6,768]{2,0,1:T(8,128)}, u32[]{:S(2)}) copy-start(f32[8,6,768]{2,0,1:T(8,128)} %param.24) | copy-start | bytes 442372
  703.5 70.0 %copy-start.42 = (f32[8,6,768]{2,0,1:T(8,128)S(1)}, f32[8,6,768]{2,0,1:T(8,128)}, u32[]{:S(2)}) copy-start(f32[8,6,768]{2,0,1:T(8,128)} %param.28) | copy-start | bytes 442372
  703.5 74.0 %copy-start.40 = (f32[2,6,2048]{2,0,1:T(2,128)S(1)}, f32[2,6,2048]{2,0,1:T(2,128)}, u32[]{:S(2)}) copy-start(f32[2,6,2048]{2,0,1:T(2,128)} %param.21) | copy-start | bytes 294916
  703.5 74.0 %copy-start.45 = (f32[2,6,2048]{2,0,1:T(2,128)S(1)}, f32[2,6,2048]{2,0,1:T(2,128)}, u32[]{:S(2)}) copy-start(f32[2,6,2048]{2,0,1:T(2,128)} %param.25) | copy-start | bytes 294916
  703.5 74.0 %copy-start.46 = (f32[2,6,2048]{2,0,1:T(2,128)S(1)}, f32[2,6,2048]{2,0,1:T(2,128)}, u32[]{:S(2)}) copy-start(f32[2,6,2048]{2,0,1:T(2,128)} %param.29) | copy-start | bytes 294916
  703.6 78.6 %copy-start.3 = (f32[16,768]{1,0:T(8,128)S(1)}, f32[16,768]{1,0:T(8,128)}, u32[]{:S(2)}) copy-start(f32[16,768]{1,0:T(8,128)} %wo.1) | copy-start | bytes 147460
  703.6 78.6 %copy-start.51 = (f32[16,768]{1,0:T(8,128)S(1)}, f32[16,768]{1,0:T(8,128)}, u32[]{:S(2)}) copy-start(f32[16,768]{1,0:T(8,128)} %param.26) | copy-start | bytes 147460
  703.6 78.6 %copy-start.52 = (f32[16,768]{1,0:T(8,128)S(1)}, f32[16,768]{1,0:T(8,128)}, u32[]{:S(2)}) copy-start(f32[16,768]{1,0:T(8,128)} %param.30) | copy-start | bytes 147460
  703.6 80.1 %copy-start.54 = (f32[3,6]{1,0:T(4,128)S(1)}, f32[3,6]{1,0:T(4,128)}, u32[]{:S(2)}) copy-start(f32[3,6]{1,0:T(4,128)} %param.23) | copy-start | bytes 220
  703.6 80.1 %copy-start.60 = (f32[3,6]{1,0:T(4,128)S(1)}, f32[3,6]{1,0:T(4,128)}, u32[]{:S(2)}) copy-start(f32[3,6]{1,0:T(4,128)} %param.27) | copy-start | bytes 220
  703.6 80.1 %copy-start.61 = (f32[3,6]{1,0:T(4,128)S(1)}, f32[3,6]{1,0:T(4,128)}, u32[]{:S(2)}) copy-start(f32[3,6]{1,0:T(4,128)} %param.31) | copy-start | bytes 220
  (2 other events, 1.2 us)
